TPU v7x, 32 devices: a whole 2x2x4 slice. The times are simulated.
32 devices in a mesh: sample: 4 (over x, core), space: 8 (over z, y).
Axes of the slice: x: 2, y: 2, z: 4, core: 2. Of those that a mesh axis runs over, the one named last changes fastest.
Arguments:
- acts: bfloat16 [8, 8, 16, 8, 8, 128], P('sample', 'space'), may hold values from -6 to 6
- weight: float32 [3456, 128], P('space'), may hold values from -0.109375 to 0.109375
- moment: float32 [3456, 128], P('space'), may hold values from -3 to 3
- second: float32 [3456, 128], P('space'), may hold values from 0.05 to 2
- cotangent: bfloat16 [8, 8, 16, 8, 8, 128], P('sample', 'space'), may hold values from -6 to 6
Outputs:
- output: bfloat16 [8, 8, 16, 8, 8, 128], P('sample', 'space')
- input_grad: bfloat16 [8, 8, 16, 8, 8, 128], P('sample', 'space')
- weight_grad: float32 [3456, 128], P('space')
- new_weight: float32 [3456, 128], P('space')
- new_moment: float32 [3456, 128], P('space')
- new_second: float32 [3456, 128], P('space')
All inputs are finite; a program needn't handle non-finite values.
Results may differ from a plain program's by a relative error of at most 0.0062.
Values may be sent and summed in bfloat16 or wider, within the bound.
A program may use at most 64 MiB of HBM per device.

v0:
```python
import jax
import jax.numpy as jnp
from jax import lax
from jax.sharding import PartitionSpec as P

GY = 2
GZ = 4


root_coef = 0.7978845608
cubic_coef = 0.044715


def shifted(value, axis, by):
    devices = lax.axis_size(axis)
    pairs = [(i, i + by) for i in range(devices) if 0 <= i + by < devices]
    return lax.ppermute(value, axis, pairs)


def convolve(field, kernel):
    return lax.conv_general_dilated(
        field,
        kernel,
        (1, 1, 1),
        "VALID",
        dimension_numbers=("NDHWC", "DHWIO", "NDHWC"),
        preferred_element_type=jnp.float32,
    )


def activate(pre):
    inner = root_coef * (pre + cubic_coef * pre * pre * pre)
    tval = jnp.tanh(inner)
    value = 0.5 * pre * (1.0 + tval)
    slope = 0.5 * (1.0 + tval) + 0.5 * pre * (1.0 - tval * tval) * root_coef * (
        1.0 + 3.0 * cubic_coef * pre * pre
    )
    return (value, slope)


def extend(field):
    place = lax.axis_index("space")
    groups = lax.axis_size("space") // (GY * GZ)
    coord_z = place % GZ
    coord_y = place // GZ % GY
    coord_x = place // (GZ * GY)
    for dim, stride, coord, count in (
        (3, 1, coord_z, GZ),
        (2, GZ, coord_y, GY),
        (1, GY * GZ, coord_x, groups),
    ):
        length = field.shape[dim]
        first_layer = lax.slice_in_dim(field, 0, 1, 1, dim)
        last_layer = lax.slice_in_dim(field, length - 1, length, 1, dim)
        below = shifted(last_layer, "space", stride)
        above = shifted(first_layer, "space", -stride)
        below = jnp.where(coord > 0, below, jnp.zeros_like(below))
        above = jnp.where(coord < count - 1, above, jnp.zeros_like(above))
        field = jnp.concatenate([below, field, above], dim)
    return field


def kernel_terms(padded, grad_pre):
    nx, ny, nz = (grad_pre.shape[1], grad_pre.shape[2], grad_pre.shape[3])
    terms = []
    for kx in range(3):
        for ky in range(3):
            for kz in range(3):
                window = padded[:, kx : kx + nx, ky : ky + ny, kz : kz + nz, :]
                terms.append(
                    lax.dot_general(
                        window,
                        grad_pre,
                        (((0, 1, 2, 3), (0, 1, 2, 3)), ((), ())),
                        preferred_element_type=jnp.float32,
                    )
                )
    stacked = jnp.stack(terms, 0)
    return stacked.reshape(27 * stacked.shape[1], stacked.shape[2])


def local(acts, weight, moment, second, cotangent):
    field = acts[:, 0]
    grad_out = cotangent[:, 0]
    channels = weight.shape[1]
    rows_bf = weight.astype(jnp.bfloat16)
    whole = lax.all_gather(rows_bf, "space", axis=0, tiled=True)
    kernel = whole.reshape(3, 3, 3, channels, channels)
    padded = extend(field)
    pre = convolve(padded, kernel)
    value, slope = activate(pre)
    output = value.astype(jnp.bfloat16)
    grad_pre = (grad_out.astype(jnp.float32) * slope).astype(jnp.bfloat16)
    flipped = jnp.flip(kernel, (0, 1, 2)).transpose(0, 1, 2, 4, 3)
    grad_padded = extend(grad_pre)
    input_grad = convolve(grad_padded, flipped).astype(jnp.bfloat16)
    total = (
        field.shape[0]
        * lax.axis_size("sample")
        * lax.axis_size("space")
        * field.shape[1]
        * field.shape[2]
        * field.shape[3]
    )
    local_terms = kernel_terms(padded, grad_pre) * float(total) ** (-0.5)
    owned = lax.psum_scatter(local_terms, "space", scatter_dimension=0, tiled=True)
    weight_grad = lax.psum(owned, "sample")
    new_moment = 0.9 * moment + 0.1 * weight_grad
    new_second = 0.999 * second + 0.001 * weight_grad * weight_grad
    first_fix = 1.0 - 0.9**10
    second_fix = 1.0 - 0.999**10
    new_weight = weight - 0.001 * (new_moment / first_fix) / (
        jnp.sqrt(new_second / second_fix) + 1e-08
    )
    return (output[:, None], input_grad[:, None], weight_grad, new_weight, new_moment, new_second)


def solution(mesh):
    in_specs = (
        P("sample", "space", None, None, None, None),
        P("space", None),
        P("space", None),
        P("space", None),
        P("sample", "space", None, None, None, None),
    )
    out_specs = (
        P("sample", "space", None, None, None, None),
        P("sample", "space", None, None, None, None),
        P("space", None),
        P("space", None),
        P("space", None),
        P("space", None),
    )
    return jax.shard_map(local, mesh=mesh, in_specs=in_specs, out_specs=out_specs, check_vma=False)
```

profile of v0, /device:TPU:0, one launch (start us, length us, event | category | flops | bytes accessed | tf_op | source)
XLA Modules:
  0.0 203.3 jit_solution(16130695142617238557)
XLA Ops:
  7.2 1.5 fusion.71
  8.7 1.3 collective-permute-start.1
  10.0 5.5 %collective-permute-start = (bf16[2,16,8,1,128]{4,3,2,1,0:T(2,128)(2,1)S(1)}, bf16[2,16,8,1,128]{4,3,2,1,0:T(2,128)(2,1)S(1)}, u32[]{:S(2)}, u32[]{:S(2)}) collective-permute-start(bf16[2,16,8,1,128]{4,3,2,1,0:T(2,128)(2,1)S(1)} %get-tuple-element.37), channel_id=1, source_target_pairs={{0,1},{1,2},{2,3},{3,4},{4,5},{5,6},{6,7},{8,9},{9,10},{10,11},{11... | collective-permute-start | bytes 196616 | tf_op jit(solution)/shard_map/ppermute | solution.py:17
  15.5 1.0 convert_element_type.18
  16.5 0.6 collective-permute-done.1
  17.2 2.8 %collective-permute-done = bf16[2,16,8,1,128]{4,3,2,1,0:T(2,128)(2,1)S(1)} collective-permute-done((bf16[2,16,8,1,128]{4,3,2,1,0:T(2,128)(2,1)S(1)}, bf16[2,16,8,1,128]{4,3,2,1,0:T(2,128)(2,1)S(1)}, u32[]{:S(2)}, u32[]{:S(2)}) %collective-permute-start) | collective-permute-done | bytes 65568 | tf_op jit(solution)/shard_map/ppermute | solution.py:17
  20.4 1.3 collective-permute-start.3
  21.7 35.9 %all_gather.3 = bf16[3456,128]{1,0:T(8,128)(2,1)S(1)} all-gather(bf16[432,128]{1,0:T(8,128)(2,1)S(1)} %convert_element_type.18), channel_id=1, replica_groups=mesh['sample'=4,'space'=8] {'space'}, dimensions={0}, use_global_device_ids=true | all-gather | bytes 995328 | tf_op jit(solution)/shard_map/all_gather | solution.py:87
  57.6 1.3 collective-permute-start.2
  58.9 2.5 %collective-permute-done.2 = bf16[2,16,1,10,128]{4,3,2,1,0:T(8,128)(2,1)S(1)} collective-permute-done((bf16[2,16,1,10,128]{4,3,2,1,0:T(8,128)(2,1)S(1)}, bf16[2,16,1,10,128]{4,3,2,1,0:T(8,128)(2,1)S(1)}, u32[]{:S(2)}, u32[]{:S(2)}) %collective-permute-start.2) | collective-permute-done | bytes 81952 | tf_op jit(solution)/shard_map/ppermute | solution.py:17
  61.5 0.7 collective-permute-start.5
  62.1 1.4 pad_maximum_fusion.3
  63.5 0.7 collective-permute-start.4
  64.2 0.7 pad_maximum_fusion
  65.0 1.5 pad_maximum_fusion.2
  66.6 6.3 %fusion.36 = f32[2,16,8,8,128]{4,0,3,2,1:T(2,128)S(1)} fusion(bf16[3,3,3,128,128]{4,3,2,1,0:T(8,128)(2,1)S(1)} %bitcast.272, bf16[2,18,10,10,128]{4,3,2,1,0:T(8,128)(2,1)S(1)} %pad_maximum_fusion), kind=kOutput, calls=%fused_computation.73 | convolution fusion | flops 1811939328 | bytes 2854912 | tf_op jit(solution)/shard_map/conv_general_dilated | solution.py:21
  72.9 1.6 fusion.34
  74.4 0.3 fusion.27
  74.8 0.4 fusion.26
  75.2 0.4 fusion.25
  75.5 0.3 fusion.24
  75.9 0.4 fusion.23
  76.3 0.4 fusion.22
  76.6 0.4 fusion.21
  77.0 0.4 fusion.20
  77.4 0.4 fusion.19
  77.8 0.3 fusion.18
  78.1 0.4 fusion.17
  78.5 0.4 fusion.16
  78.9 0.4 fusion.15
  79.3 0.3 fusion.14
  79.7 0.5 fusion.13
  80.2 0.3 fusion.12
  80.5 0.4 fusion.11
  80.9 0.4 fusion.10
  81.3 0.4 fusion.9
  81.6 0.4 fusion.8
  82.0 0.4 fusion.7
  82.4 0.4 fusion.6
  82.7 0.4 fusion.5
  83.1 0.4 fusion.4
  83.5 0.4 fusion.3
  83.9 0.4 fusion.2
  84.2 0.4 fusion.1
  84.6 1.4 broadcast_multiply_fusion
  86.1 0.2 fusion.70
  86.3 1.3 collective-permute-start.7
  87.6 4.6 %collective-permute-start.6 = (bf16[2,16,8,1,128]{4,3,2,1,0:T(2,128)(2,1)S(1)}, bf16[2,16,8,1,128]{4,3,2,1,0:T(2,128)(2,1)S(1)}, u32[]{:S(2)}, u32[]{:S(2)}) collective-permute-start(bf16[2,16,8,1,128]{4,3,2,1,0:T(2,128)(2,1)S(1)} %get-tuple-element.35), channel_id=1, source_target_pairs={{0,1},{1,2},{2,3},{3,4},{4,5},{5,6},{6,7},{8,9},{9,10},{10,11},{11... | collective-permute-start | bytes 196616 | tf_op jit(solution)/shard_map/ppermute | solution.py:17
  92.2 1.0 collective-permute-done.7
  93.3 1.3 collective-permute-done.6
  94.8 0.2 pad_maximum_fusion.10
  95.0 1.3 collective-permute-start.9
  96.3 18.0 %collective-permute-start.8 = (bf16[2,16,1,10,128]{4,3,2,1,0:T(8,128)(2,1)S(1)}, bf16[2,16,1,10,128]{4,3,2,1,0:T(8,128)(2,1)S(1)}, u32[]{:S(2)}, u32[]{:S(2)}) collective-permute-start(bf16[2,16,1,10,128]{4,3,2,1,0:T(8,128)(2,1)S(1)} %get-tuple-element.31), channel_id=1, source_target_pairs={{0,4},{1,5},{2,6},{3,7},{8,12},{9,13},{10,14},{11,15},{16,20},{17,... | collective-permute-start | bytes 245768 | tf_op jit(solution)/shard_map/ppermute | solution.py:17
  114.3 3.2 %collective-permute-done.9 = bf16[2,16,1,10,128]{4,3,2,1,0:T(8,128)(2,1)S(1)} collective-permute-done((bf16[2,16,1,10,128]{4,3,2,1,0:T(8,128)(2,1)S(1)}, bf16[2,16,1,10,128]{4,3,2,1,0:T(8,128)(2,1)S(1)}, u32[]{:S(2)}, u32[]{:S(2)}) %collective-permute-start.9) | collective-permute-done | bytes 81952 | tf_op jit(solution)/shard_map/ppermute | solution.py:17
  117.5 0.3 collective-permute-done.8
  117.9 0.7 collective-permute-start.11
  118.5 0.9 collective-permute-start.10
  119.5 0.7 pad_maximum_fusion.1
  120.2 39.6 %reduce-scatter.2.cloned.1.call-done = f32[432,128]{1,0:T(8,128)} async-done(((f32[3456,128]{1,0:T(8,128)}), f32[432,128]{1,0:T(8,128)}) %reduce-scatter.2.cloned.1.call-update) | async-done | bytes 221200 | tf_op jit(solution)/shard_map/reduce_scatter | solution.py:106
  159.9 7.3 %fusion = bf16[2,1,16,8,8,128]{5,0,4,3,2,1:T(2,128)(2,1)S(1)} fusion(bf16[3,3,3,128,128]{4,3,2,1,0:T(8,128)(2,1)} %bitcast.273, bf16[2,18,10,10,128]{4,3,2,1,0:T(8,128)(2,1)S(1)} %pad_maximum_fusion.1), kind=kOutput, calls=%fused_computation.7 | convolution fusion | flops 1812201472 | bytes 2330624 | tf_op jit(solution)/shard_map/conv_general_dilated | solution.py:21
  167.2 0.9 copy.134
  168.1 24.8 %all-reduce.2.cloned.1.call-done = f32[432,128]{1,0:T(8,128)} async-done(((f32[432,128]{1,0:T(8,128)}), f32[432,128]{1,0:T(8,128)}) %all-reduce.2.cloned.1.call-update) | async-done | bytes 221200 | tf_op jit(solution)/shard_map/psum | solution.py:107
  192.9 1.8 divide_subtract_fusion
  194.8 1.6 copy.256
  (36 shorter events, 1.2 us)
Async XLA Ops:
  7.2 13.0 %copy-start = (bf16[2,1,16,8,8,128]{5,4,3,2,1,0:T(8,128)(2,1)S(1)}, bf16[2,1,16,8,8,128]{5,4,3,2,1,0:T(8,128)(2,1)}, u32[]{:S(2)}) copy-start(bf16[2,1,16,8,8,128]{5,4,3,2,1,0:T(8,128)(2,1)} %param.5) | copy-start | bytes 1572868
  7.2 152.7 %reduce-scatter.2.cloned.1.call-start = ((), (), s32[]{:S(2)}) async-start(), calls=%async_computation.1 | async-start | bytes 1990656 | tf_op jit(solution)/shard_map/reduce_scatter | solution.py:106
  8.7 8.4 %collective-permute-start.1 = (bf16[2,16,8,1,128]{4,3,2,1,0:T(2,128)(2,1)S(1)}, bf16[2,16,8,1,128]{4,3,2,1,0:T(2,128)(2,1)S(1)}, u32[]{:S(2)}, u32[]{:S(2)}) collective-permute-start(bf16[2,16,8,1,128]{4,3,2,1,0:T(2,128)(2,1)S(1)} %get-tuple-element.38), channel_id=1, source_target_pairs={{1,0},{2,1},{3,2},{4,3},{5,4},{6,5},{7,6},{9,8},{10,9},{11,10},{12... | collective-permute-start | bytes 196616 | tf_op jit(solution)/shard_map/ppermute | solution.py:17
  10.0 10.1 %collective-permute-start = (bf16[2,16,8,1,128]{4,3,2,1,0:T(2,128)(2,1)S(1)}, bf16[2,16,8,1,128]{4,3,2,1,0:T(2,128)(2,1)S(1)}, u32[]{:S(2)}, u32[]{:S(2)}) collective-permute-start(bf16[2,16,8,1,128]{4,3,2,1,0:T(2,128)(2,1)S(1)} %get-tuple-element.37), channel_id=1, source_target_pairs={{0,1},{1,2},{2,3},{3,4},{4,5},{5,6},{6,7},{8,9},{9,10},{10,11},{11... | collective-permute-start | bytes 196616 | tf_op jit(solution)/shard_map/ppermute | solution.py:17
  20.4 38.5 %collective-permute-start.3 = (bf16[2,16,1,10,128]{4,3,2,1,0:T(8,128)(2,1)S(1)}, bf16[2,16,1,10,128]{4,3,2,1,0:T(8,128)(2,1)S(1)}, u32[]{:S(2)}, u32[]{:S(2)}) collective-permute-start(bf16[2,16,1,10,128]{4,3,2,1,0:T(8,128)(2,1)S(1)} %get-tuple-element.34), channel_id=1, source_target_pairs={{4,0},{5,1},{6,2},{7,3},{12,8},{13,9},{14,10},{15,11},{20,16},{21,... | collective-permute-start | bytes 245768 | tf_op jit(solution)/shard_map/ppermute | solution.py:17
  57.6 9.0 %copy-start.2 = (bf16[3456,128]{1,0:T(8,128)(2,1)}, bf16[3456,128]{1,0:T(8,128)(2,1)S(1)}, u32[]{:S(2)}) copy-start(bf16[3456,128]{1,0:T(8,128)(2,1)S(1)} %all_gather.3) | copy-start | bytes 2654212
  57.6 3.8 %collective-permute-start.2 = (bf16[2,16,1,10,128]{4,3,2,1,0:T(8,128)(2,1)S(1)}, bf16[2,16,1,10,128]{4,3,2,1,0:T(8,128)(2,1)S(1)}, u32[]{:S(2)}, u32[]{:S(2)}) collective-permute-start(bf16[2,16,1,10,128]{4,3,2,1,0:T(8,128)(2,1)S(1)} %get-tuple-element.33), channel_id=1, source_target_pairs={{0,4},{1,5},{2,6},{3,7},{8,12},{9,13},{10,14},{11,15},{16,20},{17,... | collective-permute-start | bytes 245768 | tf_op jit(solution)/shard_map/ppermute | solution.py:17
  61.5 2.7 %collective-permute-start.5 = (bf16[2,1,10,10,128]{4,3,2,1,0:T(8,128)(2,1)S(1)}, bf16[2,1,10,10,128]{4,3,2,1,0:T(8,128)(2,1)S(1)}, u32[]{:S(2)}, u32[]{:S(2)}) collective-permute-start(bf16[2,1,10,10,128]{4,3,2,1,0:T(8,128)(2,1)S(1)} %get-tuple-element.28), channel_id=1, source_target_pairs={} | collective-permute-start | bytes 153608 | tf_op jit(solution)/shard_map/ppermute | solution.py:17
  63.5 0.7 collective-permute-start.4
  66.5 6.3 %copy-start.3 = (bf16[2,1,16,8,8,128]{5,4,3,2,1,0:T(8,128)(2,1)S(1)}, bf16[2,1,16,8,8,128]{5,4,3,2,1,0:T(8,128)(2,1)}, u32[]{:S(2)}) copy-start(bf16[2,1,16,8,8,128]{5,4,3,2,1,0:T(8,128)(2,1)} %param.9) | copy-start | bytes 1572868
  86.1 106.9 %all-reduce.2.cloned.1.call-start = ((), (), s32[]{:S(2)}) async-start(), calls=%async_computation.2 | async-start | bytes 442368 | tf_op jit(solution)/shard_map/psum | solution.py:107
  86.3 6.9 %collective-permute-start.7 = (bf16[2,16,8,1,128]{4,3,2,1,0:T(2,128)(2,1)S(1)}, bf16[2,16,8,1,128]{4,3,2,1,0:T(2,128)(2,1)S(1)}, u32[]{:S(2)}, u32[]{:S(2)}) collective-permute-start(bf16[2,16,8,1,128]{4,3,2,1,0:T(2,128)(2,1)S(1)} %get-tuple-element.36), channel_id=1, source_target_pairs={{1,0},{2,1},{3,2},{4,3},{5,4},{6,5},{7,6},{9,8},{10,9},{11,10},{12... | collective-permute-start | bytes 196616 | tf_op jit(solution)/shard_map/ppermute | solution.py:17
  87.6 7.1 %collective-permute-start.6 = (bf16[2,16,8,1,128]{4,3,2,1,0:T(2,128)(2,1)S(1)}, bf16[2,16,8,1,128]{4,3,2,1,0:T(2,128)(2,1)S(1)}, u32[]{:S(2)}, u32[]{:S(2)}) collective-permute-start(bf16[2,16,8,1,128]{4,3,2,1,0:T(2,128)(2,1)S(1)} %get-tuple-element.35), channel_id=1, source_target_pairs={{0,1},{1,2},{2,3},{3,4},{4,5},{5,6},{6,7},{8,9},{9,10},{10,11},{11... | collective-permute-start | bytes 196616 | tf_op jit(solution)/shard_map/ppermute | solution.py:17
  95.0 22.5 %collective-permute-start.9 = (bf16[2,16,1,10,128]{4,3,2,1,0:T(8,128)(2,1)S(1)}, bf16[2,16,1,10,128]{4,3,2,1,0:T(8,128)(2,1)S(1)}, u32[]{:S(2)}, u32[]{:S(2)}) collective-permute-start(bf16[2,16,1,10,128]{4,3,2,1,0:T(8,128)(2,1)S(1)} %get-tuple-element.32), channel_id=1, source_target_pairs={{4,0},{5,1},{6,2},{7,3},{12,8},{13,9},{14,10},{15,11},{20,16},{21,... | collective-permute-start | bytes 245768 | tf_op jit(solution)/shard_map/ppermute | solution.py:17
  96.3 21.5 %collective-permute-start.8 = (bf16[2,16,1,10,128]{4,3,2,1,0:T(8,128)(2,1)S(1)}, bf16[2,16,1,10,128]{4,3,2,1,0:T(8,128)(2,1)S(1)}, u32[]{:S(2)}, u32[]{:S(2)}) collective-permute-start(bf16[2,16,1,10,128]{4,3,2,1,0:T(8,128)(2,1)S(1)} %get-tuple-element.31), channel_id=1, source_target_pairs={{0,4},{1,5},{2,6},{3,7},{8,12},{9,13},{10,14},{11,15},{16,20},{17,... | collective-permute-start | bytes 245768 | tf_op jit(solution)/shard_map/ppermute | solution.py:17
  117.9 1.6 collective-permute-start.11
  118.5 0.9 collective-permute-start.10
  159.9 33.1 %copy-start.1 = (f32[432,128]{1,0:T(8,128)S(1)}, f32[432,128]{1,0:T(8,128)}, u32[]{:S(2)}) copy-start(f32[432,128]{1,0:T(8,128)} %param.6) | copy-start | bytes 663556
  159.9 33.1 %copy-start.4 = (f32[432,128]{1,0:T(8,128)S(1)}, f32[432,128]{1,0:T(8,128)}, u32[]{:S(2)}) copy-start(f32[432,128]{1,0:T(8,128)} %param.7) | copy-start | bytes 663556
  159.9 33.1 %copy-start.5 = (f32[432,128]{1,0:T(8,128)S(1)}, f32[432,128]{1,0:T(8,128)}, u32[]{:S(2)}) copy-start(f32[432,128]{1,0:T(8,128)} %param.8) | copy-start | bytes 663556
Sparse Core Ops, SparseCore 0:
  86.2 73.5 reduce-scatter.1
  162.2 30.7 all-reduce.1
where the time goes:
time: 204 us; the launch traced here: 203 us
  waiting for transfers between devices  76.2 us (37%)
  starting transfers between devices  37.5 us (18%)
  blocking collectives  35.9 us (18%)
  matrix products  23.6 us (12%)
  between operations  14.5 us (7%)
  other arithmetic  11.4 us (6%)
  local copies, waits for them, and re-layouts  4.21 us (2%)
    reduce_scatter x1, waiting for transfers between devices, local(): lax.psum_scatter(local_terms, 'space', scatter_dimension=0, tiled=True)  39.6 us
    ppermute x12, starting transfers between devices, shifted(): return lax.ppermute(value, axis, pairs)  37.4 us
    all_gather x1, blocking collectives, local(): whole = lax.all_gather(rows_bf, 'space', axis=0, tiled=True)  35.9 us
    psum x1, waiting for transfers between devices, local(): weight_grad = lax.psum(owned, 'sample')  24.8 us
    conv_general_dilated x2, matrix products, convolve(): lax.conv_general_dilated(field, kernel, (1, 1, 1), 'VALID', dimension_num...  13.5 us
    ppermute x12, waiting for transfers between devices, shifted(): return lax.ppermute(value, axis, pairs)  11.7 us
    dot_general x27, matrix products, kernel_terms(): lax.dot_general(window, grad_pre, (((0, 1, 2, 3), (0, 1, 2, 3)), ((), ())...  10.1 us
    concatenate x4, other arithmetic, extend(): field = jnp.concatenate([below, field, above], dim)  4.4 us
  transfers between devices with their start and end apart: 14, of which 9 were waited for; matrix products, arithmetic and copies ran while one was open for 6% of the time, Pallas kernels for 0%

commit v1 on v0

--- a/solution.py
+++ b/solution.py
@@ -1,14 +1,22 @@
+import functools
+
 import jax
 import jax.numpy as jnp
 from jax import lax
+from jax.experimental import pallas as pl
+from jax.experimental.pallas import tpu as pltpu
 from jax.sharding import PartitionSpec as P
 
 GY = 2
 GZ = 4
-
+MESH = pl.DeviceIdType.MESH
+VM = pl.BlockSpec(memory_space=pltpu.VMEM)
 
 root_coef = 0.7978845608
 cubic_coef = 0.044715
+
+SIDES = (1, -1)
+DIRS = [(0, 1), (0, -1), (1, 0), (-1, 0)] + [(dy, dz) for dy in SIDES for dz in SIDES]
 
 
 def shifted(value, axis, by):
@@ -38,26 +46,297 @@
     return (value, slope)
 
 
-def extend(field):
-    place = lax.axis_index("space")
+def extend_x(field):
     groups = lax.axis_size("space") // (GY * GZ)
-    coord_z = place % GZ
-    coord_y = place // GZ % GY
-    coord_x = place // (GZ * GY)
-    for dim, stride, coord, count in (
-        (3, 1, coord_z, GZ),
-        (2, GZ, coord_y, GY),
-        (1, GY * GZ, coord_x, groups),
-    ):
-        length = field.shape[dim]
-        first_layer = lax.slice_in_dim(field, 0, 1, 1, dim)
-        last_layer = lax.slice_in_dim(field, length - 1, length, 1, dim)
-        below = shifted(last_layer, "space", stride)
-        above = shifted(first_layer, "space", -stride)
-        below = jnp.where(coord > 0, below, jnp.zeros_like(below))
-        above = jnp.where(coord < count - 1, above, jnp.zeros_like(above))
-        field = jnp.concatenate([below, field, above], dim)
-    return field
+    if groups == 1:
+        return jnp.pad(field, ((0, 0), (1, 1), (0, 0), (0, 0), (0, 0)))
+    coord = lax.axis_index("space") // (GZ * GY)
+    length = field.shape[1]
+    below = shifted(field[:, length - 1 : length], "space", GY * GZ)
+    above = shifted(field[:, :1], "space", -GY * GZ)
+    below = jnp.where(coord > 0, below, jnp.zeros_like(below))
+    above = jnp.where(coord < groups - 1, above, jnp.zeros_like(above))
+    return jnp.concatenate([below, field, above], 1)
+
+
+def faces(field):
+    ends = {1: field.shape[2] - 1, -1: 0}
+    endz = {1: field.shape[3] - 1, -1: 0}
+    zf = jnp.stack([field[:, :, :, endz[d], :] for d in SIDES])
+    yf = jnp.stack([field[:, :, ends[d], :, :] for d in SIDES])
+    cf = jnp.stack([field[:, :, ends[dy], endz[dz], :] for dy in SIDES for dz in SIDES])
+    return (zf, yf, cf)
+
+
+def assemble(field, zf, yf, cf):
+    mid = jnp.concatenate([zf[0][:, :, :, None], field, zf[1][:, :, :, None]], 3)
+    rows = []
+    for i in range(2):
+        low, high = cf[2 * i][:, :, None, :], cf[2 * i + 1][:, :, None, :]
+        rows.append(jnp.concatenate([low, yf[i], high], 2)[:, :, None])
+    return jnp.concatenate([rows[0], mid, rows[1]], 2)
+
+
+class Halo:
+    def __init__(self, ins, outs, send, recv):
+        me = lax.axis_index("space")
+        self.me, self.send, self.recv = me, send, recv
+        self.cz, self.cy = lax.rem(me, GZ), lax.rem(me // GZ, GY)
+        self.src = [ins[k // 2].at[k % 2] if k < 4 else ins[2].at[k - 4] for k in range(8)]
+        self.dst = [outs[k // 2].at[k % 2] if k < 4 else outs[2].at[k - 4] for k in range(8)]
+
+    def has(self, dy, dz):
+        y, z = self.cy + dy, self.cz + dz
+        return (y >= 0) & (y < GY) & (z >= 0) & (z < GZ)
+
+    def copy(self, k, to):
+        return pltpu.make_async_remote_copy(
+            src_ref=self.src[k],
+            dst_ref=self.dst[k],
+            send_sem=self.send.at[k],
+            recv_sem=self.recv.at[k],
+            device_id={"space": to},
+            device_id_type=MESH,
+        )
+
+    def start(self):
+        for k, (dy, dz) in enumerate(DIRS):
+
+            @pl.when(self.has(dy, dz))
+            def _():
+                self.copy(k, self.me + dy * GZ + dz).start()
+
+            @pl.when(jnp.logical_not(self.has(-dy, -dz)))
+            def _():
+                self.dst[k][...] = jnp.zeros(self.dst[k].shape, self.dst[k].dtype)
+
+    def finish(self):
+        for k, (dy, dz) in enumerate(DIRS):
+
+            @pl.when(self.has(-dy, -dz))
+            def _():
+                self.copy(k, self.me).wait_recv()
+
+            @pl.when(self.has(dy, dz))
+            def _():
+                self.copy(k, self.me).wait_send()
+
+
+def greet(n, me, sample):
+    barrier = pltpu.get_barrier_semaphore()
+
+    def space_peer(d, _):
+        pl.semaphore_signal(barrier, 1, device_id={"space": lax.rem(me + d, n)}, device_id_type=MESH)
+        return 0
+
+    lax.fori_loop(1, n, space_peer, 0)
+    for d in range(1, 4):
+        pl.semaphore_signal(barrier, 1, device_id={"sample": lax.rem(sample + d, 4)}, device_id_type=MESH)
+    pl.semaphore_wait(barrier, n + 2)
+
+
+def remote(src, dst, send, recv, **to):
+    return pltpu.make_async_remote_copy(
+        src_ref=src, dst_ref=dst, send_sem=send, recv_sem=recv, device_id=to, device_id_type=MESH
+    )
+
+
+LAG = 1
+
+
+def gather_kernel(n, w, zi, yi, ci, out, zo, yo, co, hs, hr, as_, ar, bs, br, cs, cr):
+    me, sample = lax.axis_index("space"), lax.axis_index("sample")
+    core, x = lax.rem(sample, 2), sample // 2
+    across, partner = (1 - x) * 2 + core, x * 2 + 1 - core
+    greet(n, me, sample)
+    halo = Halo((zi, yi, ci), (zo, yo, co), hs, hr)
+    halo.start()
+
+    def first(d, _):
+        o = lax.rem(me + d, n)
+        remote(w.at[core, x], out.at[me, core, x], as_.at[o], ar.at[me], space=o).start()
+        return 0
+
+    lax.fori_loop(1, n, first, 0)
+    out[me] = w[...]
+
+    def rest(t, _):
+        @pl.when(t < n)
+        def _():
+            j = lax.rem(me - t + n, n)
+            slot = out.at[j, core, x]
+            remote(slot, slot, as_.at[j], ar.at[j], space=me).wait_recv()
+            remote(slot, slot, bs.at[j], br.at[j], sample=across).start()
+
+        @pl.when(t > LAG)
+        def _():
+            j = lax.rem(me - t + LAG + n, n)
+            slot = out.at[j, core, 1 - x]
+            remote(slot, slot, bs.at[j], br.at[j], sample=across).wait_recv()
+            pair = out.at[j, core]
+            remote(pair, pair, cs.at[j], cr.at[j], sample=partner).start()
+
+        return 0
+
+    lax.fori_loop(1, n + LAG, rest, 0)
+
+    def last(d, _):
+        o = lax.rem(me + d, n)
+        pair = out.at[o, 1 - core]
+        remote(pair, pair, cs.at[o], cr.at[o], sample=partner).wait_recv()
+        remote(w.at[core, x], out.at[me, core, x], as_.at[o], ar.at[me], space=o).wait_send()
+        slot = out.at[o, core, x]
+        remote(slot, slot, bs.at[o], br.at[o], sample=across).wait_send()
+        mine = out.at[o, core]
+        remote(mine, mine, cs.at[o], cr.at[o], sample=partner).wait_send()
+        return 0
+
+    lax.fori_loop(1, n, last, 0)
+    halo.finish()
+
+
+def reduce_kernel(n, g, zi, yi, ci, out, zo, yo, co, r1, s2, r2, s3, r3, hs, hr, as_, ar, bs, br, cs, cr, ds, dr):
+    me, sample = lax.axis_index("space"), lax.axis_index("sample")
+    core, x = lax.rem(sample, 2), sample // 2
+    across, partner = (1 - x) * 2 + core, x * 2 + 1 - core
+    f32, bf16 = jnp.float32, jnp.bfloat16
+    greet(n, me, sample)
+    halo = Halo((zi, yi, ci), (zo, yo, co), hs, hr)
+    halo.start()
+
+    def owner(d):
+        return lax.rem(me + 1 + d, n)
+
+    def copy1(o):
+        return remote(g.at[o, 1 - core], r1.at[o], as_.at[o], ar.at[o], sample=partner)
+
+    def copy2(o):
+        return remote(s2.at[o, 1 - x], r2.at[o], bs.at[o], br.at[o], sample=across)
+
+    def copy3(o):
+        return remote(s3.at[o], r3.at[me], cs.at[o], cr.at[me], space=o)
+
+    def first(d, _):
+        copy1(owner(d)).start()
+        return 0
+
+    lax.fori_loop(0, n, first, 0)
+
+    def rest(t, _):
+        @pl.when(t < n)
+        def _():
+            o = owner(t)
+            copy1(o).wait_recv()
+            s2[o] = (g[o, core].astype(f32) + r1[o].astype(f32)).astype(bf16)
+            copy2(o).start()
+
+        @pl.when(t >= LAG)
+        def _():
+            o = owner(t - LAG)
+            copy2(o).wait_recv()
+            s3[o] = (s2[o, x].astype(f32) + r2[o].astype(f32)).astype(bf16)
+
+            @pl.when(t < n + LAG - 1)
+            def _():
+                copy3(o).start()
+
+        return 0
+
+    lax.fori_loop(0, n + LAG, rest, 0)
+
+    def gather(d, total):
+        j = lax.rem(me + n - d, n)
+        remote(s3.at[j], r3.at[j], cs.at[j], cr.at[j], space=j).wait_recv()
+        return total + r3[j].astype(f32)
+
+    out[core, x] = lax.fori_loop(1, n, gather, s3[me].astype(f32))
+
+    def copy4(d):
+        mine = out.at[core, x]
+        return remote(mine, mine, ds.at[d], dr.at[d], sample=lax.rem(sample + 1 + d, 4))
+
+    for d in range(3):
+        copy4(d).start()
+    for d in range(3):
+        copy4(d).wait()
+
+    def drain(d, _):
+        o = owner(d)
+        copy1(o).wait_send()
+        copy2(o).wait_send()
+
+        @pl.when(d < n - 1)
+        def _():
+            copy3(o).wait_send()
+
+        return 0
+
+    lax.fori_loop(0, n, drain, 0)
+    halo.finish()
+
+
+def quarters(value, lead):
+    rows = value.shape[-2]
+    q = -(-rows // 4)
+    if rows != 4 * q:
+        value = jnp.pad(value, [(0, 0)] * (value.ndim - 2) + [(0, 4 * q - rows), (0, 0)])
+    return value.reshape(*lead, 2, 2, q, value.shape[-1])
+
+
+def whole_rows(value, rows):
+    lead = value.shape[:-4]
+    return value.reshape(*lead, -1, value.shape[-1])[..., :rows, :]
+
+
+def like(arrays):
+    return [jax.ShapeDtypeStruct(a.shape, a.dtype) for a in arrays]
+
+
+def sems(*counts):
+    return [pltpu.SemaphoreType.DMA((c,)) for c in counts]
+
+
+def gather_weights(rows_bf, field):
+    n = lax.axis_size("space")
+    halo = faces(field)
+    w = quarters(rows_bf, ())
+    whole, zf, yf, cf = pl.pallas_call(
+        functools.partial(gather_kernel, n),
+        name="gather_and_halo",
+        out_shape=[jax.ShapeDtypeStruct((n, *w.shape), w.dtype), *like(halo)],
+        in_specs=[VM] * 4,
+        out_specs=[VM] * 4,
+        scratch_shapes=sems(8, 8, n, n, n, n, n, n),
+        compiler_params=pltpu.CompilerParams(collective_id=0, has_side_effects=True),
+    )(w, *halo)
+    whole = whole_rows(whole, rows_bf.shape[0]).reshape(-1, rows_bf.shape[1])
+    return whole, assemble(field, zf, yf, cf)
+
+
+def reduce_grads(terms, rows, field):
+    n = lax.axis_size("space")
+    halo = faces(field)
+    channels = terms.shape[-1]
+    g = quarters(terms.reshape(n, rows, channels), (n,)).astype(jnp.bfloat16)
+    q = g.shape[3]
+    bf16 = jnp.bfloat16
+    total, zf, yf, cf = pl.pallas_call(
+        functools.partial(reduce_kernel, n),
+        name="reduce_and_halo",
+        out_shape=[jax.ShapeDtypeStruct((2, 2, q, channels), jnp.float32), *like(halo)],
+        in_specs=[VM] * 4,
+        out_specs=[VM] * 4,
+        scratch_shapes=[
+            pltpu.VMEM((n, 2, q, channels), bf16),
+            pltpu.VMEM((n, 2, q, channels), bf16),
+            pltpu.VMEM((n, q, channels), bf16),
+            pltpu.VMEM((n, q, channels), bf16),
+            pltpu.VMEM((n, q, channels), bf16),
+            *sems(8, 8, n, n, n, n, n, n, 3, 3),
+        ],
+        compiler_params=pltpu.CompilerParams(collective_id=1, has_side_effects=True),
+    )(g, *halo)
+    return whole_rows(total, rows), assemble(field, zf, yf, cf)
 
 
 def kernel_terms(padded, grad_pre):
@@ -84,16 +363,13 @@
     grad_out = cotangent[:, 0]
     channels = weight.shape[1]
     rows_bf = weight.astype(jnp.bfloat16)
-    whole = lax.all_gather(rows_bf, "space", axis=0, tiled=True)
+    whole, padded = gather_weights(rows_bf, extend_x(field))
     kernel = whole.reshape(3, 3, 3, channels, channels)
-    padded = extend(field)
     pre = convolve(padded, kernel)
     value, slope = activate(pre)
     output = value.astype(jnp.bfloat16)
     grad_pre = (grad_out.astype(jnp.float32) * slope).astype(jnp.bfloat16)
     flipped = jnp.flip(kernel, (0, 1, 2)).transpose(0, 1, 2, 4, 3)
-    grad_padded = extend(grad_pre)
-    input_grad = convolve(grad_padded, flipped).astype(jnp.bfloat16)
     total = (
         field.shape[0]
         * lax.axis_size("sample")
@@ -102,9 +378,10 @@
         * field.shape[2]
         * field.shape[3]
     )
-    local_terms = kernel_terms(padded, grad_pre) * float(total) ** (-0.5)
-    owned = lax.psum_scatter(local_terms, "space", scatter_dimension=0, tiled=True)
-    weight_grad = lax.psum(owned, "sample")
+    local_terms = kernel_terms(padded, grad_pre)
+    summed, grad_padded = reduce_grads(local_terms, weight.shape[0], extend_x(grad_pre))
+    input_grad = convolve(grad_padded, flipped).astype(jnp.bfloat16)
+    weight_grad = summed * float(total) ** (-0.5)
     new_moment = 0.9 * moment + 0.1 * weight_grad
     new_second = 0.999 * second + 0.001 * weight_grad * weight_grad
     first_fix = 1.0 - 0.9**10

time: 204 us -> 100 us (0.49)
  waiting for transfers between devices: 76.2 us -> 0 us
  Pallas kernels: 0 us -> 52.6 us
  starting transfers between devices: 37.5 us -> 0 us
  blocking collectives: 35.9 us -> 0 us
  between operations: 14.5 us -> 1.02 us
  local copies, waits for them, and re-layouts: 4.21 us -> 17 us
  other arithmetic: 11.4 us -> 6.35 us
    pallas_call x0 -> x2, Pallas kernels: none -> 52.6 us  [the longest x1 27.7 us: gather_weights(): pl.pallas_call(functools.partial(gather_kernel, n), name='gather_and_halo...]
    reduce_scatter x1 -> x0, waiting for transfers between devices: 39.6 us -> none  [local(): lax.psum_scatter(local_terms, 'space', scatter_dimension=0, tiled=True)]
    ppermute x12 -> x0, starting transfers between devices: 37.4 us -> none  [shifted(): return lax.ppermute(value, axis, pairs)]
    all_gather x1 -> x0, blocking collectives: 35.9 us -> none  [local(): whole = lax.all_gather(rows_bf, 'space', axis=0, tiled=True)]
    psum x1 -> x0, waiting for transfers between devices: 24.8 us -> none  [local(): weight_grad = lax.psum(owned, 'sample')]
    ppermute x12 -> x0, waiting for transfers between devices: 11.7 us -> none  [shifted(): return lax.ppermute(value, axis, pairs)]
    another operation x0 -> x15, local copies, waits for them, and re-layouts: none -> 5.18 us  [the longest x4 1.51 us: faces(): zf = jnp.stack([field[:, :, :, endz[d], :] for d in SIDES])]
    concatenate x4, other arithmetic: 4.4 us -> 1.65 us  [the longest x3 0.89 us: assemble(): return jnp.concatenate([rows[0], mid, rows[1]], 2)]
  transfers between devices with their start and end apart: 14 -> 0, of which waited for: 9 -> 0; matrix products, arithmetic and copies ran while one was open for 6% -> 0% of each run, Pallas kernels for 0% -> 0%
where the time goes in v1:
time: 100 us; the launch traced here: 99.7 us
  Pallas kernels  52.6 us (53%)
  matrix products  22.7 us (23%)
  local copies, waits for them, and re-layouts  17 us (17%)
  other arithmetic  6.35 us (6%)
  between operations  1.02 us (1%)
    pallas_call x1, Pallas kernels, gather_weights(): pl.pallas_call(functools.partial(gather_kernel, n), name='gather_and_halo...  27.7 us
    pallas_call x1, Pallas kernels, reduce_grads(): pl.pallas_call(functools.partial(reduce_kernel, n), name='reduce_and_halo...  24.9 us
    conv_general_dilated x2, matrix products, convolve(): lax.conv_general_dilated(field, kernel, (1, 1, 1), 'VALID', dimension_num...  12.5 us
    dot_general x27, matrix products, kernel_terms(): lax.dot_general(window, grad_pre, (((0, 1, 2, 3), (0, 1, 2, 3)), ((), ())...  10.2 us
    unnamed x23, local copies, waits for them, and re-layouts  5.08 us
    slice x3, local copies, waits for them, and re-layouts, kernel_terms(): window = padded[:, kx:kx + nx, ky:ky + ny, kz:kz + nz, :]  2.33 us

profile of v1, /device:TPU:0, one launch (start us, length us, event | category | flops | bytes accessed | tf_op | source)
XLA Modules:
  0.0 99.7 jit_solution(4206470748296325839)
XLA Ops:
  0.6 1.0 convert_element_type.24
  1.6 0.7 reshape.25.w
  2.3 1.4 %copy.326 = bf16[2,1,16,8,8,128]{5,2,0,4,3,1:T(8,128)(2,1)S(1)} copy(bf16[2,1,16,8,8,128]{5,4,3,2,1,0:T(8,128)(2,1)} %param.5) | data formatting | bytes 1048576 | tf_op args[0]
  3.6 0.1 fusion.128
  3.7 0.7 copy.94.zi
  4.4 0.1 fusion.130
  4.5 0.7 copy.95.yi
  5.2 0.6 pad_maximum_fusion.9.ci
  5.9 27.7 %gather_and_halo.1 = (bf16[8,2,2,108,128]{4,3,2,1,0:T(8,128)(2,1)}, bf16[2,2,18,8,128]{4,3,2,1,0:T(8,128)(2,1)}, bf16[2,2,18,8,128]{4,3,2,1,0:T(8,128)(2,1)}, bf16[4,2,18,128]{3,2,1,0:T(8,128)(2,1)}) custom-call(bf16[2,2,108,128]{3,2,1,0:T(8,128)(2,1)} %reshape.25.w, bf16[2,2,18,8,128]{4,3,2,1,0:T(8,128)(2,1)} %copy.94.zi, ...), custom_call_target="tpu_custom_call" | custom-call | tf_op jit(solution)/shard_map/gather_and_halo/pallas_call | solution.py:303
  33.6 1.3 %reshape_reshape_reshape.4 = bf16[3,3,3,128,128]{4,3,2,1,0:T(8,128)(2,1)S(1)} reshape(bf16[8,2,2,108,128]{4,3,2,1,0:T(8,128)(2,1)} %get-tuple-element.17) | data formatting | bytes 1769472 | tf_op jit(solution)/shard_map/reshape;reshape;reshape | solution.py:367
  35.1 0.3 pad.7
  35.4 0.3 pad_maximum_fusion
  35.7 6.3 %fusion.90 = f32[2,16,8,8,128]{4,0,3,2,1:T(2,128)S(1)} fusion(bf16[3,3,3,128,128]{4,3,2,1,0:T(8,128)(2,1)S(1)} %reshape_reshape_reshape.4, bf16[2,18,10,10,128]{4,1,0,3,2:T(8,128)(2,1)S(1)} %pad_maximum_fusion), kind=kOutput, calls=%fused_computation.129 | convolution fusion | flops 1811939328 | bytes 2854912 | tf_op jit(solution)/shard_map/conv_general_dilated | solution.py:29
  42.0 1.3 %fusion.88 = (bf16[2,16,8,8,128]{4,1,0,3,2:T(8,128)(2,1)S(1)}, bf16[2,1,16,8,8,128]{5,2,0,4,3,1:T(8,128)(2,1)S(1)}) fusion(f32[2,16,8,8,128]{4,0,3,2,1:T(2,128)S(1)} %fusion.90, bf16[2,1,16,8,8,128]{5,4,3,2,1,0:T(8,128)(2,1)S(1)} %copy-done.2), kind=kLoop, calls=%fused_computation.126 | loop fusion | flops 5767168 | bytes 2621440 | tf_op jit(solution)/shard_map/convert_element_type | solution.py:371
  43.4 1.0 %copy.171 = bf16[2,1,16,8,8,128]{5,4,3,2,1,0:T(8,128)(2,1)} copy(bf16[2,1,16,8,8,128]{5,2,0,4,3,1:T(8,128)(2,1)S(1)} %get-tuple-element.56) | data formatting | bytes 1048576
  44.3 0.4 pad_maximum_fusion.2
  44.7 1.0 fusion.168
  45.7 0.3 fusion.81
  46.0 0.4 fusion.79
  46.4 0.4 fusion.77
  46.8 0.8 pad_maximum_fusion.3
  47.5 0.4 fusion.75
  47.9 0.4 pad_slice_fusion.8
  48.3 0.4 fusion.73
  48.7 0.4 fusion.71
  49.1 0.9 fusion.167
  50.0 0.4 fusion.69
  50.4 0.4 fusion.67
  50.7 0.4 fusion.65
  51.1 0.4 fusion.63
  51.5 0.4 fusion.61
  51.8 0.4 fusion.59
  52.2 0.4 fusion.57
  52.6 0.7 copy-done.3
  53.2 0.6 fusion.55
  53.8 0.4 fusion.53
  54.2 0.4 fusion.51
  54.5 0.4 fusion.49
  54.9 0.4 fusion.47
  55.3 0.4 fusion.45
  55.6 0.4 fusion.43
  56.0 0.4 fusion.41
  56.4 0.4 fusion.39
  56.7 0.6 fusion.37
  57.3 0.4 fusion.35
  57.7 0.4 fusion.33
  58.1 0.4 fusion.31
  58.4 0.4 fusion.29
  58.8 1.1 %convert_element_type.29.g = bf16[8,2,2,108,128]{4,3,2,1,0:T(8,128)(2,1)} reshape(bf16[27,128,128]{2,1,0:T(8,128)(2,1)S(1)} %fusion.29) | data formatting | bytes 1769472 | tf_op jit(solution)/shard_map/convert_element_type | solution.py:320
  60.0 0.7 copy.164.zi
  60.8 0.7 copy.165.yi
  61.5 0.6 pad_maximum_fusion.10.ci
  62.1 24.9 %reduce_and_halo.1 = (f32[2,2,108,128]{3,2,1,0:T(8,128)}, bf16[2,2,18,8,128]{4,3,2,1,0:T(8,128)(2,1)}, bf16[2,2,18,8,128]{4,3,2,1,0:T(8,128)(2,1)}, bf16[4,2,18,128]{3,2,1,0:T(8,128)(2,1)}) custom-call(bf16[8,2,2,108,128]{4,3,2,1,0:T(8,128)(2,1)} %convert_element_type.29.g, bf16[2,2,18,8,128]{4,3,2,1,0:T(8,128)(2,1)} %copy.164.zi, ...), custom_call_target="tpu_custom_call" | custom-call | tf_op jit(solution)/shard_map/reduce_and_halo/pallas_call | solution.py:323
  87.0 0.8 slice_bitcast_fusion.11
  87.8 0.9 copy.166
  88.8 0.9 copy.167
  89.8 0.3 pad.8
  90.1 0.3 pad_maximum_fusion.1
  90.4 6.2 %fusion = bf16[2,1,16,8,8,128]{5,0,4,3,2,1:T(2,128)(2,1)S(1)} fusion(bf16[3,3,3,128,128]{4,3,2,1,0:T(8,128)(2,1)S(1)} %reshape_reshape_reshape.4, bf16[2,18,10,10,128]{4,1,0,3,2:T(8,128)(2,1)S(1)} %pad_maximum_fusion.1), kind=kOutput, calls=%fused_computation.3 | convolution fusion | flops 1812201472 | bytes 2330624 | tf_op jit(solution)/shard_map/conv_general_dilated | solution.py:29
  96.6 0.9 copy.172
  97.7 0.8 copy-done.1
  98.4 0.2 copy-done.5
  98.6 0.1 copy-done.6
  98.7 0.9 divide_subtract_fusion
  (38 shorter events, 0.6 us)
Async XLA Ops:
  33.5 1.4 %copy-start.9 = (bf16[4,2,18,128]{3,2,1,0:T(8,128)(2,1)S(1)}, bf16[4,2,18,128]{3,2,1,0:T(8,128)(2,1)}, u32[]{:S(2)}) copy-start(bf16[4,2,18,128]{3,2,1,0:T(8,128)(2,1)} %get-tuple-element.14) | copy-start | bytes 110596
  33.6 1.4 %copy-start.8 = (bf16[2,2,18,8,128]{4,3,2,1,0:T(8,128)(2,1)S(1)}, bf16[2,2,18,8,128]{4,3,2,1,0:T(8,128)(2,1)}, u32[]{:S(2)}) copy-start(bf16[2,2,18,8,128]{4,3,2,1,0:T(8,128)(2,1)} %get-tuple-element.15) | copy-start | bytes 442372
  33.6 1.5 %copy-start.7 = (bf16[2,2,18,8,128]{4,3,2,1,0:T(8,128)(2,1)S(1)}, bf16[2,2,18,8,128]{4,3,2,1,0:T(8,128)(2,1)}, u32[]{:S(2)}) copy-start(bf16[2,2,18,8,128]{4,3,2,1,0:T(8,128)(2,1)} %get-tuple-element.16) | copy-start | bytes 442372
  35.7 6.3 %copy-start.2 = (bf16[2,1,16,8,8,128]{5,4,3,2,1,0:T(8,128)(2,1)S(1)}, bf16[2,1,16,8,8,128]{5,4,3,2,1,0:T(8,128)(2,1)}, u32[]{:S(2)}) copy-start(bf16[2,1,16,8,8,128]{5,4,3,2,1,0:T(8,128)(2,1)} %param.9) | copy-start | bytes 1572868
  52.2 1.0 %copy-start.3 = (bf16[2,1,16,8,8,128]{5,4,3,2,1,0:T(8,128)(2,1)S(1)}, bf16[2,1,16,8,8,128]{5,4,3,2,1,0:T(8,128)(2,1)}, u32[]{:S(2)}) copy-start(bf16[2,1,16,8,8,128]{5,4,3,2,1,0:T(8,128)(2,1)} %param.5) | copy-start | bytes 1572868
  90.4 7.1 %copy-start.4 = (f32[2,2,108,128]{3,2,1,0:T(8,128)S(1)}, f32[2,2,108,128]{3,2,1,0:T(8,128)}, u32[]{:S(2)}) copy-start(f32[2,2,108,128]{3,2,1,0:T(8,128)} %get-tuple-element.21) | copy-start | bytes 663556
  97.5 0.9 copy-start.1
  97.5 1.1 %copy-start.5 = (f32[432,128]{1,0:T(8,128)S(1)}, f32[432,128]{1,0:T(8,128)}, u32[]{:S(2)}) copy-start(f32[432,128]{1,0:T(8,128)} %param.7) | copy-start | bytes 663556
  97.5 1.2 %copy-start.6 = (f32[432,128]{1,0:T(8,128)S(1)}, f32[432,128]{1,0:T(8,128)}, u32[]{:S(2)}) copy-start(f32[432,128]{1,0:T(8,128)} %param.8) | copy-start | bytes 663556
  97.6 2.1 %copy-start = (f32[432,128]{1,0:T(8,128)}, f32[432,128]{1,0:T(8,128)S(1)}, u32[]{:S(2)}) copy-start(f32[432,128]{1,0:T(8,128)S(1)} %mul.113) | copy-start | bytes 663556

commit v2 on v1

--- a/solution.py
+++ b/solution.py
@@ -141,7 +141,7 @@
     )
 
 
-LAG = 1
+LAG = 6
 
 
 def gather_kernel(n, w, zi, yi, ci, out, zo, yo, co, hs, hr, as_, ar, bs, br, cs, cr):
@@ -340,22 +340,15 @@
 
 
 def kernel_terms(padded, grad_pre):
-    nx, ny, nz = (grad_pre.shape[1], grad_pre.shape[2], grad_pre.shape[3])
-    terms = []
-    for kx in range(3):
-        for ky in range(3):
-            for kz in range(3):
-                window = padded[:, kx : kx + nx, ky : ky + ny, kz : kz + nz, :]
-                terms.append(
-                    lax.dot_general(
-                        window,
-                        grad_pre,
-                        (((0, 1, 2, 3), (0, 1, 2, 3)), ((), ())),
-                        preferred_element_type=jnp.float32,
-                    )
-                )
-    stacked = jnp.stack(terms, 0)
-    return stacked.reshape(27 * stacked.shape[1], stacked.shape[2])
+    terms = lax.conv_general_dilated(
+        padded,
+        grad_pre,
+        (1, 1, 1),
+        "VALID",
+        dimension_numbers=("CDHWN", "IDHWO", "DHWNC"),
+        preferred_element_type=jnp.float32,
+    )
+    return terms.reshape(-1, terms.shape[-1])
 
 
 def local(acts, weight, moment, second, cotangent):

time: 100 us -> 89.9 us (0.90)
  Pallas kernels: 52.6 us -> 43.4 us
    dot_general x27 -> x0, matrix products: 10.2 us -> none  [kernel_terms(): lax.dot_general(window, grad_pre, (((0, 1, 2, 3), (0, 1, 2, 3)), ((), ())...]
    conv_general_dilated x0 -> x1, matrix products: none -> 8.95 us  [kernel_terms(): lax.conv_general_dilated(padded, grad_pre, (1, 1, 1), 'VALID', dimension_...]
    pallas_call x1, Pallas kernels: 27.7 us -> 22.9 us  [gather_weights(): pl.pallas_call(functools.partial(gather_kernel, n), name='gather_and_halo...]
    pallas_call x1, Pallas kernels: 24.9 us -> 20.5 us  [reduce_grads(): pl.pallas_call(functools.partial(reduce_kernel, n), name='reduce_and_halo...]
    slice x3 -> x0, local copies, waits for them, and re-layouts: 2.33 us -> none  [kernel_terms(): window = padded[:, kx:kx + nx, ky:ky + ny, kz:kz + nz, :]]
    conv_general_dilated x2, matrix products: 12.5 us -> 13.8 us  [convolve(): lax.conv_general_dilated(field, kernel, (1, 1, 1), 'VALID', dimension_num...]
    unnamed x23 -> x25, local copies, waits for them, and re-layouts: 5.08 us -> 6.22 us
where the time goes in v2:
time: 89.9 us; the launch traced here: 89.5 us
  Pallas kernels  43.4 us (48%)
  matrix products  22.8 us (25%)
  local copies, waits for them, and re-layouts  16.4 us (18%)
  other arithmetic  6 us (7%)
  between operations  0.94 us (1%)
    pallas_call x1, Pallas kernels, gather_weights(): pl.pallas_call(functools.partial(gather_kernel, n), name='gather_and_halo...  22.9 us
    pallas_call x1, Pallas kernels, reduce_grads(): pl.pallas_call(functools.partial(reduce_kernel, n), name='reduce_and_halo...  20.5 us
    conv_general_dilated x2, matrix products, convolve(): lax.conv_general_dilated(field, kernel, (1, 1, 1), 'VALID', dimension_num...  13.8 us
    conv_general_dilated x1, matrix products, kernel_terms(): lax.conv_general_dilated(padded, grad_pre, (1, 1, 1), 'VALID', dimension_...  8.95 us
    unnamed x25, local copies, waits for them, and re-layouts  6.22 us
    convert_element_type x1, other arithmetic, local(): grad_pre = (grad_out.astype(jnp.float32) * slope).astype(jnp.bfloat16)  2.1 us

profile of v2, /device:TPU:0, one launch (start us, length us, event | category | flops | bytes accessed | tf_op | source)
XLA Modules:
  0.0 89.5 jit_solution(8828402456523709968)
XLA Ops:
  0.6 1.0 %convert_element_type.26 = bf16[432,128]{1,0:T(8,128)(2,1)S(1)} convert(f32[432,128]{1,0:T(8,128)} %param.6) | non-fusion elementwise | flops 55296 | bytes 331776 | tf_op jit(solution)/shard_map/convert_element_type | solution.py:358
  1.6 0.7 reshape.25.w
  2.3 1.4 %copy.90 = bf16[2,1,16,8,8,128]{5,2,0,4,3,1:T(8,128)(2,1)S(1)} copy(bf16[2,1,16,8,8,128]{5,4,3,2,1,0:T(8,128)(2,1)} %param.5) | data formatting | bytes 1048576 | tf_op args[0]
  3.7 0.6 pad_maximum_fusion.6.ci
  4.3 0.1 fusion.14
  4.4 0.7 copy.42.zi
  5.1 0.1 fusion.16
  5.2 0.7 copy.43.yi
  5.9 0.3 pad.7
  6.2 22.9 %gather_and_halo.1 = (bf16[8,2,2,108,128]{4,3,2,1,0:T(8,128)(2,1)}, bf16[2,2,18,8,128]{4,3,2,1,0:T(8,128)(2,1)}, bf16[2,2,18,8,128]{4,3,2,1,0:T(8,128)(2,1)}, bf16[4,2,18,128]{3,2,1,0:T(8,128)(2,1)}) custom-call(bf16[2,2,108,128]{3,2,1,0:T(8,128)(2,1)} %reshape.25.w, bf16[2,2,18,8,128]{4,3,2,1,0:T(8,128)(2,1)} %copy.42.zi, ...), custom_call_target="tpu_custom_call" | custom-call | tf_op jit(solution)/shard_map/gather_and_halo/pallas_call | solution.py:303
  29.1 0.0 copy-start.9
  29.1 0.8 slice_bitcast_fusion.15
  29.9 0.9 %copy.44 = bf16[2,2,18,8,128]{4,2,1,3,0:T(8,128)(2,1)S(1)} copy(bf16[2,2,18,8,128]{4,3,2,1,0:T(8,128)(2,1)} %get-tuple-element.15) | data formatting | bytes 294912 | tf_op jit(solution)/shard_map/gather_and_halo/pallas_call | solution.py:303
  30.9 0.0 copy-done.9
  31.0 0.0 copy-start.1
  31.0 0.3 pad_maximum_fusion
  31.3 0.9 %copy-done.1 = bf16[8,2,2,108,128]{4,3,2,1,0:T(8,128)(2,1)S(1)} copy-done((bf16[8,2,2,108,128]{4,3,2,1,0:T(8,128)(2,1)S(1)}, bf16[8,2,2,108,128]{4,3,2,1,0:T(8,128)(2,1)}, u32[]{:S(2)}) %copy-start.1) | copy-done | bytes 884760
  32.2 1.1 %reshape_reshape_reshape.4 = bf16[3,3,3,128,128]{4,3,2,1,0:T(8,128)(2,1)} reshape(bf16[8,2,2,108,128]{4,3,2,1,0:T(8,128)(2,1)S(1)} %copy-done.1) | data formatting | bytes 1769472 | tf_op jit(solution)/shard_map/reshape;reshape;reshape | solution.py:360
  33.3 0.0 copy-start.5
  33.3 7.5 %fusion.12 = f32[2,16,8,8,128]{4,0,3,2,1:T(2,128)S(1)} fusion(bf16[3,3,3,128,128]{4,3,2,1,0:T(8,128)(2,1)} %reshape_reshape_reshape.4, bf16[2,18,10,10,128]{4,1,0,3,2:T(8,128)(2,1)S(1)} %pad_maximum_fusion), kind=kOutput, calls=%fused_computation.20 | convolution fusion | flops 1811939328 | bytes 2854912 | tf_op jit(solution)/shard_map/conv_general_dilated | solution.py:29
  40.8 0.0 copy-done.5
  40.8 2.1 %fusion.7 = (bf16[2,16,8,8,128]{4,1,0,3,2:T(8,128)(2,1)S(1)}, bf16[2,1,16,8,8,128]{5,2,0,4,3,1:T(8,128)(2,1)}) fusion(f32[2,16,8,8,128]{4,0,3,2,1:T(2,128)S(1)} %fusion.12, bf16[2,1,16,8,8,128]{5,4,3,2,1,0:T(8,128)(2,1)S(1)} %copy-done.5), kind=kLoop, calls=%fused_computation.13 | loop fusion | flops 5767168 | bytes 2621440 | tf_op jit(solution)/shard_map/convert_element_type | solution.py:364
  42.9 0.0 copy-start
  42.9 9.0 %convolution_convert_fusion = bf16[3,3,3,128,128]{4,3,2,1,0:T(8,128)(2,1)S(1)} fusion(bf16[2,16,8,8,128]{4,1,0,3,2:T(8,128)(2,1)S(1)} %get-tuple-element.37, bf16[2,18,10,10,128]{4,1,0,3,2:T(8,128)(2,1)S(1)} %pad_maximum_fusion), kind=kOutput, calls=%fused_computation.2 | convolution fusion | flops 1812381696 | bytes 2330624 | tf_op jit(solution)/shard_map/conv_general_dilated | solution.py:343
  51.8 0.0 copy-done
  51.8 1.0 %copy.67 = bf16[2,1,16,8,8,128]{5,4,3,2,1,0:T(8,128)(2,1)} copy(bf16[2,1,16,8,8,128]{5,2,0,4,3,1:T(8,128)(2,1)S(1)} %copy-done) | data formatting | bytes 1048576
  52.8 1.1 %convert_element_type.32.g = bf16[8,2,2,108,128]{4,3,2,1,0:T(8,128)(2,1)} reshape(bf16[3,3,3,128,128]{4,3,2,1,0:T(8,128)(2,1)S(1)} %convolution_convert_fusion) | data formatting | bytes 1769472 | tf_op jit(solution)/shard_map/convert_element_type | solution.py:320
  54.0 0.6 pad_maximum_fusion.7.ci
  54.6 0.1 fusion.18
  54.7 0.7 copy.60.zi
  55.4 0.1 fusion.20
  55.5 0.7 copy.61.yi
  56.2 20.5 %reduce_and_halo.1 = (f32[2,2,108,128]{3,2,1,0:T(8,128)}, bf16[2,2,18,8,128]{4,3,2,1,0:T(8,128)(2,1)}, bf16[2,2,18,8,128]{4,3,2,1,0:T(8,128)(2,1)}, bf16[4,2,18,128]{3,2,1,0:T(8,128)(2,1)}) custom-call(bf16[8,2,2,108,128]{4,3,2,1,0:T(8,128)(2,1)} %convert_element_type.32.g, bf16[2,2,18,8,128]{4,3,2,1,0:T(8,128)(2,1)} %copy.60.zi, ...), custom_call_target="tpu_custom_call" | custom-call | tf_op jit(solution)/shard_map/reduce_and_halo/pallas_call | solution.py:323
  76.7 0.0 copy-start.10
  76.7 0.8 slice_bitcast_fusion.11
  77.5 0.9 %copy.62 = bf16[2,2,18,8,128]{4,2,1,3,0:T(8,128)(2,1)S(1)} copy(bf16[2,2,18,8,128]{4,3,2,1,0:T(8,128)(2,1)} %get-tuple-element.19) | data formatting | bytes 294912 | tf_op jit(solution)/shard_map/reduce_and_halo/pallas_call | solution.py:323
  78.6 0.0 copy-done.10
  78.6 0.3 pad.8
  78.9 0.0 copy-start.2
  78.9 0.3 pad_maximum_fusion.1
  79.2 0.9 %copy-done.2 = bf16[3,3,3,128,128]{4,3,2,1,0:T(8,128)(2,1)S(1)} copy-done((bf16[3,3,3,128,128]{4,3,2,1,0:T(8,128)(2,1)S(1)}, bf16[3,3,3,128,128]{4,3,2,1,0:T(8,128)(2,1)}, u32[]{:S(2)}) %copy-start.2) | copy-done | bytes 884760
  80.1 0.0 copy-start.6
  80.1 6.3 %fusion = bf16[2,1,16,8,8,128]{5,0,4,3,2,1:T(2,128)(2,1)S(1)} fusion(bf16[3,3,3,128,128]{4,3,2,1,0:T(8,128)(2,1)S(1)} %copy-done.2, bf16[2,18,10,10,128]{4,1,0,3,2:T(8,128)(2,1)S(1)} %pad_maximum_fusion.1), kind=kOutput, calls=%fused_computation.4 | convolution fusion | flops 1812201472 | bytes 2330624 | tf_op jit(solution)/shard_map/conv_general_dilated | solution.py:29
  86.4 0.9 %copy.68 = bf16[2,1,16,8,8,128]{5,4,3,2,1,0:T(8,128)(2,1)} copy(bf16[2,1,16,8,8,128]{5,0,4,3,2,1:T(2,128)(2,1)S(1)} %fusion) | data formatting | bytes 1048576
  87.4 0.0 copy-done.6
  87.4 0.0 copy-start.4
  87.4 0.0 copy-start.7
  87.4 0.0 copy-start.8
  87.5 0.0 copy-start.3
  87.5 0.8 copy-done.4
  88.3 0.2 copy-done.7
  88.5 0.1 copy-done.8
  88.6 0.9 %divide_subtract_fusion = (f32[432,128]{1,0:T(8,128)}, f32[432,128]{1,0:T(8,128)}, f32[432,128]{1,0:T(8,128)}) fusion(f32[432,128]{1,0:T(8,128)S(1)} %copy-done.4, f32[432,128]{1,0:T(8,128)S(1)} %mul.118, f32[432,128]{1,0:T(8,128)S(1)} %copy-done.7, f32[432,128]{1,0:T(8,128)S(1)} %mul.125, f32[432,128]{1,0:T(8,128)S(1)} %mul.113, f32[432,128]{1,0:T(8,128)S(1)} %copy-done.8), kind=kLoop, calls=%fused_computation.38 | loop fusion | flops 552960 | bytes 1990656 | tf_op jit(solution)/shard_map/sub | solution.py:382
  89.5 0.0 copy-done.3
  (19 shorter events, 0.5 us)
Async XLA Ops:
  29.1 1.8 %copy-start.9 = (bf16[2,2,18,8,128]{4,3,2,1,0:T(8,128)(2,1)S(1)}, bf16[2,2,18,8,128]{4,3,2,1,0:T(8,128)(2,1)}, u32[]{:S(2)}) copy-start(bf16[2,2,18,8,128]{4,3,2,1,0:T(8,128)(2,1)} %get-tuple-element.16) | copy-start | bytes 442372
  31.0 1.2 %copy-start.1 = (bf16[8,2,2,108,128]{4,3,2,1,0:T(8,128)(2,1)S(1)}, bf16[8,2,2,108,128]{4,3,2,1,0:T(8,128)(2,1)}, u32[]{:S(2)}) copy-start(bf16[8,2,2,108,128]{4,3,2,1,0:T(8,128)(2,1)} %get-tuple-element.17) | copy-start | bytes 2654212
  33.3 7.5 %copy-start.5 = (bf16[2,1,16,8,8,128]{5,4,3,2,1,0:T(8,128)(2,1)S(1)}, bf16[2,1,16,8,8,128]{5,4,3,2,1,0:T(8,128)(2,1)}, u32[]{:S(2)}) copy-start(bf16[2,1,16,8,8,128]{5,4,3,2,1,0:T(8,128)(2,1)} %param.9) | copy-start | bytes 1572868
  42.9 9.0 %copy-start = (bf16[2,1,16,8,8,128]{5,2,0,4,3,1:T(8,128)(2,1)S(1)}, bf16[2,1,16,8,8,128]{5,2,0,4,3,1:T(8,128)(2,1)}, u32[]{:S(2)}) copy-start(bf16[2,1,16,8,8,128]{5,2,0,4,3,1:T(8,128)(2,1)} %get-tuple-element.38) | copy-start | bytes 1572868
  76.7 1.9 %copy-start.10 = (bf16[2,2,18,8,128]{4,3,2,1,0:T(8,128)(2,1)S(1)}, bf16[2,2,18,8,128]{4,3,2,1,0:T(8,128)(2,1)}, u32[]{:S(2)}) copy-start(bf16[2,2,18,8,128]{4,3,2,1,0:T(8,128)(2,1)} %get-tuple-element.20) | copy-start | bytes 442372
  78.9 1.2 %copy-start.2 = (bf16[3,3,3,128,128]{4,3,2,1,0:T(8,128)(2,1)S(1)}, bf16[3,3,3,128,128]{4,3,2,1,0:T(8,128)(2,1)}, u32[]{:S(2)}) copy-start(bf16[3,3,3,128,128]{4,3,2,1,0:T(8,128)(2,1)} %reshape_reshape_reshape.4) | copy-start | bytes 2654212
  80.1 7.3 %copy-start.6 = (f32[2,2,108,128]{3,2,1,0:T(8,128)S(1)}, f32[2,2,108,128]{3,2,1,0:T(8,128)}, u32[]{:S(2)}) copy-start(f32[2,2,108,128]{3,2,1,0:T(8,128)} %get-tuple-element.21) | copy-start | bytes 663556
  87.4 0.9 %copy-start.4 = (f32[432,128]{1,0:T(8,128)S(1)}, f32[432,128]{1,0:T(8,128)}, u32[]{:S(2)}) copy-start(f32[432,128]{1,0:T(8,128)} %param.6) | copy-start | bytes 663556
  87.4 1.1 %copy-start.7 = (f32[432,128]{1,0:T(8,128)S(1)}, f32[432,128]{1,0:T(8,128)}, u32[]{:S(2)}) copy-start(f32[432,128]{1,0:T(8,128)} %param.7) | copy-start | bytes 663556
  87.4 1.2 %copy-start.8 = (f32[432,128]{1,0:T(8,128)S(1)}, f32[432,128]{1,0:T(8,128)}, u32[]{:S(2)}) copy-start(f32[432,128]{1,0:T(8,128)} %param.8) | copy-start | bytes 663556
  87.5 2.0 %copy-start.3 = (f32[432,128]{1,0:T(8,128)}, f32[432,128]{1,0:T(8,128)S(1)}, u32[]{:S(2)}) copy-start(f32[432,128]{1,0:T(8,128)S(1)} %mul.113) | copy-start | bytes 663556
